TPU v7x, 32 devices: a whole 2x2x4 slice. The times are simulated.
32 devices in a mesh: lat: 8 (over y, x, core), lon: 4 (over z).
Axes of the slice: x: 2, y: 2, z: 4, core: 2. Of those that a mesh axis runs over, the one named last changes fastest.
Arguments:
- tracers: float32 [4, 4, 256, 720], P(None, None, 'lat', 'lon'), may hold values from -6 to 6
- courant: float32 [2, 4, 256, 720], P(None, None, 'lat', 'lon'), may hold values from -0.8 to 0.8
- cutoffs: int32 [256], replicated, may hold values from 1 to 360, as said below
Outputs:
- updated: float32 [4, 4, 256, 720], P(None, None, 'lat', 'lon')
- filtered_zonal: float32 [4, 256, 720], P(None, 'lat', 'lon')
Inputs may be any that keep to these rules, and one draw needn't show every extreme that they name: cutoffs[j] is 360 for every row j with min(j, 255 - j) >= 64, below 360 for all other rows, and 1 at the two pole rows.
All inputs are finite; a program needn't handle non-finite values.
Results may differ from a plain program's by a relative error of at most 0.0003.
Values sent between devices are 32-bit elements; how exact they have to be, the bound alone decides.
A program may use at most 64 MiB of HBM per device.

v0:
```python
import math
import jax
import jax.numpy as jnp
from jax import lax
from jax.sharding import PartitionSpec as P


def padded(cells, sides, width, closed):
    for axis, dim in sides:
        count = lax.axis_size(axis)
        ends = count if closed else count - 1
        head = lax.slice_in_dim(cells, 0, width, axis=dim)
        tail = lax.slice_in_dim(cells, cells.shape[dim] - width, cells.shape[dim], axis=dim)
        cells = jnp.concatenate(
            [
                lax.ppermute(tail, axis, [(i, (i + 1) % count) for i in range(ends)]),
                cells,
                lax.ppermute(head, axis, [((i + 1) % count, i) for i in range(ends)]),
            ],
            axis=dim,
        )
    return cells


def take_range(values, start, count, axis_index):
    return lax.slice_in_dim(values, start, start + count, axis=axis_index)


def ppm_flux(extended, courant_faces, axis_index):
    cell_count = extended.shape[axis_index] - 6
    edge_values = 7.0 / 12.0 * (
        take_range(extended, 1, cell_count + 3, axis_index)
        + take_range(extended, 2, cell_count + 3, axis_index)
    ) - 1.0 / 12.0 * (
        take_range(extended, 0, cell_count + 3, axis_index)
        + take_range(extended, 3, cell_count + 3, axis_index)
    )
    left_edge = take_range(edge_values, 0, cell_count + 2, axis_index)
    right_edge = take_range(edge_values, 1, cell_count + 2, axis_index)
    centre = take_range(extended, 2, cell_count + 2, axis_index)
    slopes = right_edge - left_edge
    curvature = 6.0 * centre - 3.0 * (left_edge + right_edge)
    upwind = take_range(right_edge, 0, cell_count + 1, axis_index) - 0.5 * courant_faces * (
        take_range(slopes, 0, cell_count + 1, axis_index)
        - (1.0 - courant_faces * (2.0 / 3.0)) * take_range(curvature, 0, cell_count + 1, axis_index)
    )
    downwind = take_range(left_edge, 1, cell_count + 1, axis_index) - 0.5 * courant_faces * (
        take_range(slopes, 1, cell_count + 1, axis_index)
        + (1.0 + courant_faces * (2.0 / 3.0)) * take_range(curvature, 1, cell_count + 1, axis_index)
    )
    return courant_faces * jnp.where(courant_faces > 0, upwind, downwind)


def metric_weights(first_row, row_count, grid_rows):
    faces = first_row + jnp.arange(-1, row_count, dtype=jnp.int32)
    centres = first_row + jnp.arange(row_count, dtype=jnp.int32)
    face_weight = jnp.sin(
        jnp.minimum(faces + 1, grid_rows - 1 - faces).astype(jnp.float32) * (math.pi / grid_rows)
    )
    cell_weight = jnp.sin(
        (jnp.minimum(centres, grid_rows - 1 - centres).astype(jnp.float32) + 0.5)
        * (math.pi / grid_rows)
    )
    return (face_weight, cell_weight)


def angle_table(first_ids, second_ids, period):
    product = first_ids[:, None] * second_ids[None, :] % period
    angles = product.astype(jnp.float32) * (2.0 * math.pi / period)
    return (jnp.cos(angles), jnp.sin(angles))


def spectral_lowpass(row_block, limits, outer_count):
    row_count, circle = row_block.shape
    inner_count = circle // outer_count
    highest = lax.Precision.HIGHEST
    grid_values = row_block.reshape(row_count, outer_count, inner_count)
    outer_ids = jnp.arange(outer_count, dtype=jnp.int32)
    inner_ids = jnp.arange(inner_count, dtype=jnp.int32)
    outer_cos, outer_sin = angle_table(outer_ids, outer_ids, outer_count)
    inner_cos, inner_sin = angle_table(inner_ids, inner_ids, inner_count)
    twiddle_cos, twiddle_sin = angle_table(inner_ids, outer_ids, circle)
    first_real = jnp.einsum("rab,ak->rbk", grid_values, outer_cos, precision=highest)
    first_imag = -jnp.einsum("rab,ak->rbk", grid_values, outer_sin, precision=highest)
    turned_real = first_real * twiddle_cos + first_imag * twiddle_sin
    turned_imag = first_imag * twiddle_cos - first_real * twiddle_sin
    coeff_real = jnp.einsum("rbk,bj->rjk", turned_real, inner_cos, precision=highest) + jnp.einsum(
        "rbk,bj->rjk", turned_imag, inner_sin, precision=highest
    )
    coeff_imag = jnp.einsum("rbk,bj->rjk", turned_imag, inner_cos, precision=highest) - jnp.einsum(
        "rbk,bj->rjk", turned_real, inner_sin, precision=highest
    )
    wavenumber = inner_ids[:, None] * outer_count + outer_ids[None, :]
    folded = jnp.minimum(wavenumber, circle - wavenumber)
    keep_mask = folded[None, :, :] <= limits[:, None, None]
    coeff_real = jnp.where(keep_mask, coeff_real, 0.0)
    coeff_imag = jnp.where(keep_mask, coeff_imag, 0.0)
    back_real = jnp.einsum("rjk,jb->rbk", coeff_real, inner_cos, precision=highest) - jnp.einsum(
        "rjk,jb->rbk", coeff_imag, inner_sin, precision=highest
    )
    back_imag = jnp.einsum("rjk,jb->rbk", coeff_imag, inner_cos, precision=highest) + jnp.einsum(
        "rjk,jb->rbk", coeff_real, inner_sin, precision=highest
    )
    reverted_real = back_real * twiddle_cos - back_imag * twiddle_sin
    reverted_imag = back_imag * twiddle_cos + back_real * twiddle_sin
    signal = jnp.einsum("rbk,ka->rab", reverted_real, outer_cos, precision=highest) - jnp.einsum(
        "rbk,ka->rab", reverted_imag, outer_sin, precision=highest
    )
    return (signal / circle).reshape(row_count, circle)


def circle_filter(row_block, limits, lon_groups):
    row_count = row_block.shape[0]
    whole_rows = lax.all_to_all(row_block, "lon", split_axis=0, concat_axis=1, tiled=True)
    held_count = row_count // lon_groups
    row_limits = lax.dynamic_slice_in_dim(limits, lax.axis_index("lon") * held_count, held_count)
    lowpass = spectral_lowpass(whole_rows, row_limits, lon_groups)
    lowpass = jnp.where((row_limits < whole_rows.shape[1] // 2)[:, None], lowpass, whole_rows)
    return lax.all_to_all(lowpass, "lon", split_axis=1, concat_axis=0, tiled=True)


def body(tracers, courant, cutoffs):
    levels, tracer_count, lat_rows, lon_cols = tracers.shape
    lon_groups = lax.axis_size("lon")
    lat_bands = lax.axis_size("lat")
    band_index = lax.axis_index("lat")
    grid_rows = lat_rows * lat_bands
    zonal = courant[0]
    meridional = courant[1]
    lat_stack = jnp.concatenate([tracers, meridional[:, None]], axis=1)
    lat_ext = padded(lat_stack, (("lat", 2),), 3, False)
    flat_count = levels * lat_rows
    flat_zonal = zonal.reshape(flat_count, lon_cols)
    local_limits = lax.dynamic_slice_in_dim(cutoffs, band_index * lat_rows, lat_rows)
    filtered_flat = circle_filter(flat_zonal, jnp.tile(local_limits, levels), lon_groups)
    filtered_zonal = filtered_flat.reshape(levels, lat_rows, lon_cols)
    lon_stack = jnp.concatenate([tracers, filtered_zonal[:, None]], axis=1)
    lon_ext = padded(lon_stack, (("lon", 3),), 3, True)
    flux_east = ppm_flux(
        lon_ext[:, :tracer_count], lon_ext[:, tracer_count:, :, 2 : lon_cols + 3], 3
    )
    face_weight, cell_weight = metric_weights(band_index * lat_rows, lat_rows, grid_rows)
    flux_north = (
        ppm_flux(lat_ext[:, :tracer_count], lat_ext[:, tracer_count:, 2 : lat_rows + 3, :], 2)
        * face_weight[None, None, :, None]
    )
    change = (
        flux_east[:, :, :, 1:]
        - flux_east[:, :, :, :-1]
        + (flux_north[:, :, 1:, :] - flux_north[:, :, :-1, :]) / cell_weight[None, None, :, None]
    )
    return (tracers - change, filtered_zonal)


def solution(mesh):
    in_specs = (P(None, None, "lat", "lon"), P(None, None, "lat", "lon"), P())
    out_specs = (P(None, None, "lat", "lon"), P(None, "lat", "lon"))
    return jax.shard_map(body, mesh=mesh, in_specs=in_specs, out_specs=out_specs, check_vma=False)
```

profile of v0, /device:TPU:0, one launch (start us, length us, event | category | flops | bytes accessed | tf_op | source)
XLA Modules:
  0.0 59.9 jit_solution(16525917794037167420)
XLA Ops:
  0.6 0.0 copy-start
  0.6 1.7 %slice_bitcast_fusion.1 = (f32[4,32,180]{2,1,0:T(8,128)}, f32[4,1,32,180]{3,2,1,0:T(8,128)S(1)}) fusion(f32[2,4,32,180]{3,2,1,0:T(8,128)} %param.4), kind=kLoop, calls=%fused_computation.113 | loop fusion | bytes 368640 | tf_op jit(solution)/shard_map/all_to_all | solution.py:114
  2.3 0.0 copy-done
  2.4 1.3 %collective-permute-start.3 = (f32[4,5,3,180]{3,2,1,0:T(4,128)S(1)}, f32[4,5,3,180]{3,2,1,0:T(4,128)S(1)}, u32[]{:S(2)}, u32[]{:S(2)}) collective-permute-start(f32[4,5,3,180]{3,2,1,0:T(4,128)S(1)} %get-tuple-element.15), channel_id=1, source_target_pairs={{4,0},{8,4},{12,8},{16,12},{20,16},{24,20},{28,24},{5,1},{9,5},{13... | collective-permute-start | bytes 129608 | tf_op jit(solution)/shard_map/ppermute | solution.py:18
  3.7 3.0 %collective-permute-start.2 = (f32[4,5,3,180]{3,2,1,0:T(4,128)S(1)}, f32[4,5,3,180]{3,2,1,0:T(4,128)S(1)}, u32[]{:S(2)}, u32[]{:S(2)}) collective-permute-start(f32[4,5,3,180]{3,2,1,0:T(4,128)S(1)} %get-tuple-element.14), channel_id=1, source_target_pairs={{0,4},{4,8},{8,12},{12,16},{16,20},{20,24},{24,28},{1,5},{5,9},{9,... | collective-permute-start | bytes 129608 | tf_op jit(solution)/shard_map/ppermute | solution.py:16
  6.7 6.4 %all-to-all-start = ((f32[4,32,180]{2,1,0:T(8,128)}), f32[4,32,180]{2,1,0:T(8,128)S(1)}, u32[]{:S(2)}, u32[]{:S(2)}) async-start(f32[4,32,180]{2,1,0:T(8,128)} %get-tuple-element.22), calls=%async_computation | async-start | bytes 262144 | tf_op jit(solution)/shard_map/all_to_all | solution.py:114
  13.1 0.1 fusion.114
  13.2 0.0 copy-start.1
  13.2 0.7 %copy-done.1 = s32[256]{0:T(256)S(1)} copy-done((s32[256]{0:T(256)S(1)}, s32[256]{0:T(256)}, u32[]{:S(2)}) %copy-start.1) | copy-done | bytes 1048
  13.9 0.1 dynamic_slice.6
  14.0 0.1 tile.10
  14.1 0.1 broadcast_compare_fusion
  14.2 0.0 collective-permute-done.3
  14.2 0.0 collective-permute-done.2
  14.2 0.1 pad_maximum_fusion
  14.3 0.3 fusion.20
  14.6 0.2 slice_subtract_fusion
  14.9 4.8 %all-to-all-done = f32[4,32,180]{2,1,0:T(8,128)S(1)} async-done(((f32[4,32,180]{2,1,0:T(8,128)}), f32[4,32,180]{2,1,0:T(8,128)S(1)}, u32[]{:S(2)}, u32[]{:S(2)}) %all-to-all-start) | async-done | bytes 92192 | tf_op jit(solution)/shard_map/all_to_all | solution.py:114
  19.7 0.4 convolution_bitcast_fusion
  20.1 0.4 multiply_add_fusion
  20.6 1.0 %fusion.47 = f32[180,32,4]{0,1,2:T(8,128)S(1)} fusion(f32[32,180,4]{1,2,0:T(4,128)S(1)} %get-tuple-element.21), kind=kOutput, calls=%fused_computation.82 | convolution fusion | flops 50058000 | bytes 184320 | tf_op jit(solution)/shard_map/rbk,bj->rjk/dot_general | solution.py:90
  21.6 1.0 %fusion.51 = f32[180,32,4]{0,1,2:T(8,128)S(1)} fusion(f32[32,180,4]{1,2,0:T(4,128)S(1)} %get-tuple-element.20), kind=kOutput, calls=%fused_computation.86 | convolution fusion | flops 50058000 | bytes 184320 | tf_op jit(solution)/shard_map/rbk,bj->rjk/dot_general | solution.py:87
  22.7 1.1 %fusion.5 = f32[32,180,4]{1,0,2:T(8,128)S(1)} fusion(f32[180,32,4]{0,1,2:T(8,128)S(1)} %fusion.47, f32[32,180,4]{1,2,0:T(4,128)S(1)} %get-tuple-element.20, s32[180,4]{0,1:T(4,128)S(1)} %subtract_minimum_fusion, s32[32]{0:T(128)S(1)} %get-tuple-element.7), kind=kOutput, calls=%fused_computation.11 | convolution fusion | flops 50127120 | bytes 279488 | tf_op jit(solution)/shard_map/rbk,bj->rjk/dot_general | solution.py:90
  23.8 1.1 %fusion.45 = f32[180,32,4]{0,1,2:T(8,128)S(1)} fusion(f32[32,180,4]{1,0,2:T(8,128)S(1)} %fusion.5), kind=kOutput, calls=%fused_computation.80 | convolution fusion | flops 50058000 | bytes 184320 | tf_op jit(solution)/shard_map/rjk,jb->rbk/dot_general | solution.py:101
  24.8 1.0 %fusion.7 = f32[32,180,4]{1,0,2:T(8,128)S(1)} fusion(f32[180,32,4]{0,1,2:T(8,128)S(1)} %fusion.51, f32[32,180,4]{1,2,0:T(4,128)S(1)} %get-tuple-element.21, s32[180,4]{0,1:T(4,128)S(1)} %subtract_minimum_fusion, s32[32]{0:T(128)S(1)} %get-tuple-element.7), kind=kOutput, calls=%fused_computation.14 | convolution fusion | flops 50127120 | bytes 279488 | tf_op jit(solution)/shard_map/rbk,bj->rjk/dot_general | solution.py:87
  25.9 1.0 %fusion.49 = f32[180,32,4]{0,1,2:T(8,128)S(1)} fusion(f32[32,180,4]{1,0,2:T(8,128)S(1)} %fusion.7), kind=kOutput, calls=%fused_computation.84 | convolution fusion | flops 50058000 | bytes 184320 | tf_op jit(solution)/shard_map/rjk,jb->rbk/dot_general | solution.py:98
  26.9 1.1 %convolution_add_fusion = f32[180,32,4]{0,1,2:T(8,128)S(1)} fusion(f32[180,32,4]{0,1,2:T(8,128)S(1)} %fusion.45, f32[32,180,4]{1,0,2:T(8,128)S(1)} %fusion.7), kind=kOutput, calls=%fused_computation.7 | convolution fusion | flops 50081040 | bytes 276480 | tf_op jit(solution)/shard_map/rjk,jb->rbk/dot_general | solution.py:101
  28.0 1.1 %add_bitcast_fusion.2 = (f32[32,180,4]{1,0,2:T(8,128)S(1)}, f32[32,180,4]{1,0,2:T(8,128)S(1)}) fusion(f32[180,32,4]{0,1,2:T(8,128)S(1)} %convolution_add_fusion, f32[180,4]{0,1:T(4,128)S(1)} %get-tuple-element.30, f32[180,4]{0,1:T(4,128)S(1)} %get-tuple-element.31, f32[180,32,4]{0,1,2:T(8,128)S(1)} %fusion.49, f32[32,180,4]{1,0,2:T(8,128)S(1)} %fusion.5), kind=kOutput, calls=%fused_computation.109 | convolution fusion | flops 50219280 | bytes 466560 | tf_op jit(solution)/shard_map/rjk,jb->rbk/dot_general | solution.py:98
  29.0 0.4 fusion.69
  29.5 0.5 fusion.3
  30.0 0.7 %copy.21 = f32[32,4,180]{2,0,1:T(8,128)} copy(f32[32,4,180]{2,1,0:T(4,128)S(1)} %fusion.3) | data formatting | bytes 184320 | tf_op jit(solution)/shard_map/jit(_where)/select_n | solution.py:118
  30.6 3.4 %all-to-all-start.1 = ((f32[32,4,180]{2,0,1:T(8,128)}), f32[32,4,180]{2,0,1:T(8,128)S(1)}, u32[]{:S(2)}, u32[]{:S(2)}) async-start(f32[32,4,180]{2,0,1:T(8,128)} %copy.21), calls=%async_computation.1 | async-start | bytes 262144 | tf_op jit(solution)/shard_map/all_to_all | solution.py:119
  34.1 6.2 %all-to-all-done.1 = f32[32,4,180]{2,0,1:T(8,128)S(1)} async-done(((f32[32,4,180]{2,0,1:T(8,128)}), f32[32,4,180]{2,0,1:T(8,128)S(1)}, u32[]{:S(2)}, u32[]{:S(2)}) %all-to-all-start.1) | async-done | bytes 92192 | tf_op jit(solution)/shard_map/all_to_all | solution.py:119
  40.3 0.2 fusion.38
  40.4 1.7 %collective-permute-start.1 = (f32[4,5,32,3]{3,2,1,0:T(8,128)S(1)}, f32[4,5,32,3]{3,2,1,0:T(8,128)S(1)}, u32[]{:S(2)}, u32[]{:S(2)}) collective-permute-start(f32[4,5,32,3]{3,2,1,0:T(8,128)S(1)} %get-tuple-element.11), channel_id=1, source_target_pairs={{1,0},{2,1},{3,2},{0,3},{5,4},{6,5},{7,6},{4,7},{9,8},{10,9},{11,1... | collective-permute-start | bytes 23048 | tf_op jit(solution)/shard_map/ppermute | solution.py:18
  42.1 0.4 collective-permute-start
  42.5 0.4 fusion.13
  42.9 7.3 %collective-permute-done.1 = f32[4,5,32,3]{3,2,1,0:T(8,128)S(1)} collective-permute-done((f32[4,5,32,3]{3,2,1,0:T(8,128)S(1)}, f32[4,5,32,3]{3,2,1,0:T(8,128)S(1)}, u32[]{:S(2)}, u32[]{:S(2)}) %collective-permute-start.1) | collective-permute-done | bytes 7712 | tf_op jit(solution)/shard_map/ppermute | solution.py:18
  50.2 6.2 %collective-permute-done = f32[4,5,32,3]{3,2,1,0:T(8,128)S(1)} collective-permute-done((f32[4,5,32,3]{3,2,1,0:T(8,128)S(1)}, f32[4,5,32,3]{3,2,1,0:T(8,128)S(1)}, u32[]{:S(2)}, u32[]{:S(2)}) %collective-permute-start) | collective-permute-done | bytes 7712 | tf_op jit(solution)/shard_map/ppermute | solution.py:16
  56.4 0.3 pad_maximum_fusion.5
  56.7 0.5 fusion.36
  57.3 0.3 slice_subtract_fusion.3
  57.6 0.1 compare_bitcast_fusion.1
  57.8 0.5 fusion.29
  58.3 1.0 %fusion.24 = f32[4,4,32,180]{3,2,1,0:T(8,128)} fusion(f32[4,4,32,180]{3,2,1,0:T(8,128)S(1)} %copy-done, f32[4,4,33,180]{3,2,1,0:T(8,128)S(1)} %fusion.13, f32[4,4,32,181]{3,2,1,0:T(8,128)S(1)} %fusion.29, f32[32]{0:T(128)S(1)} %fusion.125), kind=kLoop, calls=%fused_computation.47 | loop fusion | flops 460800 | bytes 2211968 | tf_op jit(solution)/shard_map/sub | solution.py:152
  59.3 0.7 %copy.47 = f32[4,32,180]{2,1,0:T(8,128)} copy(f32[4,32,180]{2,1,0:T(8,128)S(1)} %bitcast.95) | data formatting | bytes 184320
  (9 shorter events, 0.3 us)
Async XLA Ops:
  0.6 1.7 %copy-start = (f32[4,4,32,180]{3,2,1,0:T(8,128)S(1)}, f32[4,4,32,180]{3,2,1,0:T(8,128)}, u32[]{:S(2)}) copy-start(f32[4,4,32,180]{3,2,1,0:T(8,128)} %param.3) | copy-start | bytes 1105924
  2.4 11.8 %collective-permute-start.3 = (f32[4,5,3,180]{3,2,1,0:T(4,128)S(1)}, f32[4,5,3,180]{3,2,1,0:T(4,128)S(1)}, u32[]{:S(2)}, u32[]{:S(2)}) collective-permute-start(f32[4,5,3,180]{3,2,1,0:T(4,128)S(1)} %get-tuple-element.15), channel_id=1, source_target_pairs={{4,0},{8,4},{12,8},{16,12},{20,16},{24,20},{28,24},{5,1},{9,5},{13... | collective-permute-start | bytes 129608 | tf_op jit(solution)/shard_map/ppermute | solution.py:18
  3.7 10.5 %collective-permute-start.2 = (f32[4,5,3,180]{3,2,1,0:T(4,128)S(1)}, f32[4,5,3,180]{3,2,1,0:T(4,128)S(1)}, u32[]{:S(2)}, u32[]{:S(2)}) collective-permute-start(f32[4,5,3,180]{3,2,1,0:T(4,128)S(1)} %get-tuple-element.14), channel_id=1, source_target_pairs={{0,4},{4,8},{8,12},{12,16},{16,20},{20,24},{24,28},{1,5},{5,9},{9,... | collective-permute-start | bytes 129608 | tf_op jit(solution)/shard_map/ppermute | solution.py:16
  6.7 13.0 %all-to-all-start = ((f32[4,32,180]{2,1,0:T(8,128)}), f32[4,32,180]{2,1,0:T(8,128)S(1)}, u32[]{:S(2)}, u32[]{:S(2)}) async-start(f32[4,32,180]{2,1,0:T(8,128)} %get-tuple-element.22), calls=%async_computation | async-start | bytes 262144 | tf_op jit(solution)/shard_map/all_to_all | solution.py:114
  13.2 0.7 %copy-start.1 = (s32[256]{0:T(256)S(1)}, s32[256]{0:T(256)}, u32[]{:S(2)}) copy-start(s32[256]{0:T(256)} %param.5) | copy-start | bytes 3076
  30.6 9.6 %all-to-all-start.1 = ((f32[32,4,180]{2,0,1:T(8,128)}), f32[32,4,180]{2,0,1:T(8,128)S(1)}, u32[]{:S(2)}, u32[]{:S(2)}) async-start(f32[32,4,180]{2,0,1:T(8,128)} %copy.21), calls=%async_computation.1 | async-start | bytes 262144 | tf_op jit(solution)/shard_map/all_to_all | solution.py:119
  40.4 9.8 %collective-permute-start.1 = (f32[4,5,32,3]{3,2,1,0:T(8,128)S(1)}, f32[4,5,32,3]{3,2,1,0:T(8,128)S(1)}, u32[]{:S(2)}, u32[]{:S(2)}) collective-permute-start(f32[4,5,32,3]{3,2,1,0:T(8,128)S(1)} %get-tuple-element.11), channel_id=1, source_target_pairs={{1,0},{2,1},{3,2},{0,3},{5,4},{6,5},{7,6},{4,7},{9,8},{10,9},{11,1... | collective-permute-start | bytes 23048 | tf_op jit(solution)/shard_map/ppermute | solution.py:18
  42.1 14.3 %collective-permute-start = (f32[4,5,32,3]{3,2,1,0:T(8,128)S(1)}, f32[4,5,32,3]{3,2,1,0:T(8,128)S(1)}, u32[]{:S(2)}, u32[]{:S(2)}) collective-permute-start(f32[4,5,32,3]{3,2,1,0:T(8,128)S(1)} %get-tuple-element.10), channel_id=1, source_target_pairs={{0,1},{1,2},{2,3},{3,0},{4,5},{5,6},{6,7},{7,4},{8,9},{9,10},{10,1... | collective-permute-start | bytes 23048 | tf_op jit(solution)/shard_map/ppermute | solution.py:16
where the time goes:
time: 60.3 us; the launch traced here: 59.9 us
  waiting for transfers between devices  24.5 us (41%)
  starting transfers between devices  16.2 us (27%)
  matrix products  10.1 us (17%)
  other arithmetic  4.35 us (7%)
  local copies, waits for them, and re-layouts  3.88 us (6%)
  between operations  0.88 us (1%)
    ppermute x2, waiting for transfers between devices, padded(): lax.ppermute(head, axis, [((i + 1) % count, i) for i in range(ends)])  7.29 us
    all_to_all x1, starting transfers between devices, circle_filter(): lax.all_to_all(row_block, 'lon', split_axis=0, concat_axis=1, tiled=True)  6.36 us
    ppermute x2, waiting for transfers between devices, padded(): lax.ppermute(tail, axis, [(i, (i + 1) % count) for i in range(ends)])  6.19 us
    all_to_all x1, waiting for transfers between devices, circle_filter(): lax.all_to_all(lowpass, 'lon', split_axis=1, concat_axis=0, tiled=True)  6.16 us
    all_to_all x1, waiting for transfers between devices, circle_filter(): lax.all_to_all(row_block, 'lon', split_axis=0, concat_axis=1, tiled=True)  4.84 us
    ppermute x2, starting transfers between devices, padded(): lax.ppermute(tail, axis, [(i, (i + 1) % count) for i in range(ends)])  3.45 us
    all_to_all x1, starting transfers between devices, circle_filter(): lax.all_to_all(lowpass, 'lon', split_axis=1, concat_axis=0, tiled=True)  3.43 us
    ppermute x2, starting transfers between devices, padded(): lax.ppermute(head, axis, [((i + 1) % count, i) for i in range(ends)])  2.95 us
  transfers between devices with their start and end apart: 6, of which 4 were waited for; matrix products, arithmetic and copies ran while one was open for 2% of the time, Pallas kernels for 0%

commit v1 on v0

--- a/solution.py
+++ b/solution.py
@@ -3,6 +3,17 @@
 import jax.numpy as jnp
 from jax import lax
 from jax.sharding import PartitionSpec as P
+
+
+def in_blocks(x, dim, size):
+    before, after = (x.shape[:dim], x.shape[dim + 1 :])
+    return jnp.moveaxis(x.reshape(*before, size, -1, *after), dim, 0)
+
+
+def in_order(blocks, dim):
+    blocks = jnp.moveaxis(blocks, 0, dim)
+    shape = blocks.shape
+    return blocks.reshape(*shape[:dim], shape[dim] * shape[dim + 1], *shape[dim + 2 :])
 
 
 def padded(cells, sides, width, closed):
@@ -111,7 +122,14 @@
 
 def circle_filter(row_block, limits, lon_groups):
     row_count = row_block.shape[0]
-    whole_rows = lax.all_to_all(row_block, "lon", split_axis=0, concat_axis=1, tiled=True)
+    size, place = (lax.axis_size("lon"), lax.axis_index("lon"))
+    blocks = in_blocks(row_block, 0, size)
+    outs = [blocks[place]]
+    for step in range(1, size):
+        sent = blocks[place ^ step]
+        outs.append(lax.ppermute(sent, "lon", [(i_2, i_2 ^ step) for i_2 in range(size)]))
+    blocks = jnp.stack(outs)[place ^ jnp.arange(size)]
+    whole_rows = in_order(blocks, 1)
     held_count = row_count // lon_groups
     row_limits = lax.dynamic_slice_in_dim(limits, lax.axis_index("lon") * held_count, held_count)
     lowpass = spectral_lowpass(whole_rows, row_limits, lon_groups)

time: 60.3 us -> 57.6 us (0.955)
  waiting for transfers between devices: 24.5 us -> 22.4 us
  starting transfers between devices: 16.2 us -> 15.5 us
    all_to_all x1 -> x0, starting transfers between devices: 6.36 us -> none  [circle_filter(): lax.all_to_all(row_block, 'lon', split_axis=0, concat_axis=1, tiled=True)]
    ppermute x0 -> x3, starting transfers between devices: none -> 5.78 us  [circle_filter(): lax.ppermute(sent, 'lon', [(i_2, i_2 ^ step) for i_2 in range(size)])]
    all_to_all x1 -> x0, waiting for transfers between devices: 4.84 us -> none  [circle_filter(): lax.all_to_all(row_block, 'lon', split_axis=0, concat_axis=1, tiled=True)]
    ppermute x0 -> x3, waiting for transfers between devices: none -> 3.24 us  [circle_filter(): lax.ppermute(sent, 'lon', [(i_2, i_2 ^ step) for i_2 in range(size)])]
    all_to_all x1 -> x0, local copies, waits for them, and re-layouts: 1.7 us -> none  [circle_filter(): lax.all_to_all(row_block, 'lon', split_axis=0, concat_axis=1, tiled=True)]
    slice x0 -> x1, local copies, waits for them, and re-layouts: none -> 1.04 us  [body(): zonal = courant[0]]
  transfers between devices with their start and end apart: 6 -> 8, of which waited for: 4 -> 5; matrix products, arithmetic and copies ran while one was open for 2% -> 23% of each run, Pallas kernels for 0% -> 0%
where the time goes in v1:
time: 57.6 us; the launch traced here: 57.3 us
  waiting for transfers between devices  22.4 us (39%)
  starting transfers between devices  15.5 us (27%)
  matrix products  10.2 us (18%)
  other arithmetic  4.38 us (8%)
  local copies, waits for them, and re-layouts  3.9 us (7%)
  between operations  0.95 us (2%)
    ppermute x2, waiting for transfers between devices, padded(): lax.ppermute(head, axis, [((i + 1) % count, i) for i in range(ends)])  7.29 us
    ppermute x2, waiting for transfers between devices, padded(): lax.ppermute(tail, axis, [(i, (i + 1) % count) for i in range(ends)])  6.26 us
    ppermute x3, starting transfers between devices, circle_filter(): lax.ppermute(sent, 'lon', [(i_2, i_2 ^ step) for i_2 in range(size)])  5.78 us
    all_to_all x1, waiting for transfers between devices, circle_filter(): lax.all_to_all(lowpass, 'lon', split_axis=1, concat_axis=0, tiled=True)  5.58 us
    ppermute x2, starting transfers between devices, padded(): lax.ppermute(tail, axis, [(i, (i + 1) % count) for i in range(ends)])  3.45 us
    all_to_all x1, starting transfers between devices, circle_filter(): lax.all_to_all(lowpass, 'lon', split_axis=1, concat_axis=0, tiled=True)  3.33 us
    ppermute x3, waiting for transfers between devices, circle_filter(): lax.ppermute(sent, 'lon', [(i_2, i_2 ^ step) for i_2 in range(size)])  3.24 us
    ppermute x2, starting transfers between devices, padded(): lax.ppermute(head, axis, [((i + 1) % count, i) for i in range(ends)])  2.95 us
  transfers between devices with their start and end apart: 8, of which 5 were waited for; matrix products, arithmetic and copies ran while one was open for 23% of the time, Pallas kernels for 0%

profile of v1, /device:TPU:0, one launch (start us, length us, event | category | flops | bytes accessed | tf_op | source)
XLA Modules:
  0.0 57.3 jit_solution(9671600675421786162)
XLA Ops:
  0.6 1.0 %fusion.164 = (f32[1,4,32,180]{3,2,1,0:T(8,128)S(1)}, f32[4,1,32,180]{3,2,1,0:T(8,128)S(1)}) fusion(f32[2,4,32,180]{3,2,1,0:T(8,128)} %param.4), kind=kLoop, calls=%fused_computation.213 | loop fusion | bytes 368640 | tf_op jit(solution)/shard_map/slice | solution.py:146
  1.7 0.1 copy-done
  1.8 1.3 %collective-permute-start.6 = (f32[4,5,3,180]{3,2,1,0:T(4,128)S(1)}, f32[4,5,3,180]{3,2,1,0:T(4,128)S(1)}, u32[]{:S(2)}, u32[]{:S(2)}) collective-permute-start(f32[4,5,3,180]{3,2,1,0:T(4,128)S(1)} %get-tuple-element.17), channel_id=1, source_target_pairs={{4,0},{8,4},{12,8},{16,12},{20,16},{24,20},{28,24},{5,1},{9,5},{13... | collective-permute-start | bytes 129608 | tf_op jit(solution)/shard_map/ppermute | solution.py:29
  3.1 3.0 %collective-permute-start.5 = (f32[4,5,3,180]{3,2,1,0:T(4,128)S(1)}, f32[4,5,3,180]{3,2,1,0:T(4,128)S(1)}, u32[]{:S(2)}, u32[]{:S(2)}) collective-permute-start(f32[4,5,3,180]{3,2,1,0:T(4,128)S(1)} %get-tuple-element.16), channel_id=1, source_target_pairs={{0,4},{4,8},{8,12},{12,16},{16,20},{20,24},{24,28},{1,5},{5,9},{9,... | collective-permute-start | bytes 129608 | tf_op jit(solution)/shard_map/ppermute | solution.py:27
  6.2 5.1 %collective-permute-start.2 = (f32[32,180]{1,0:T(8,128)S(1)}, f32[32,180]{1,0:T(8,128)S(1)}, u32[]{:S(2)}, u32[]{:S(2)}) collective-permute-start(f32[32,180]{1,0:T(8,128)S(1)} %get-tuple-element.31), channel_id=1, source_target_pairs={{0,3},{1,2},{2,1},{3,0},{4,7},{5,6},{6,5},{7,4},{8,11},{9,10},{10,... | collective-permute-start | bytes 69128 | tf_op jit(solution)/shard_map/ppermute | solution.py:130
  11.4 0.0 collective-permute-start.1
  11.4 0.6 %collective-permute-start = (f32[32,180]{1,0:T(8,128)S(1)}, f32[32,180]{1,0:T(8,128)S(1)}, u32[]{:S(2)}, u32[]{:S(2)}) collective-permute-start(f32[32,180]{1,0:T(8,128)S(1)} %get-tuple-element.33), channel_id=1, source_target_pairs={{0,1},{1,0},{2,3},{3,2},{4,5},{5,4},{6,7},{7,6},{8,9},{9,8},{10,11... | collective-permute-start | bytes 69128 | tf_op jit(solution)/shard_map/ppermute | solution.py:130
  12.0 0.1 fusion.111
  12.2 0.0 copy-start.1
  12.2 0.7 %copy-done.1 = s32[256]{0:T(256)S(1)} copy-done((s32[256]{0:T(256)S(1)}, s32[256]{0:T(256)}, u32[]{:S(2)}) %copy-start.1) | copy-done | bytes 1048
  12.9 0.1 dynamic_slice.20
  12.9 0.1 tile.10
  13.0 0.1 broadcast_compare_fusion
  13.2 0.2 collective-permute-done.2
  13.4 3.0 %collective-permute-done.1 = f32[32,180]{1,0:T(8,128)S(1)} collective-permute-done((f32[32,180]{1,0:T(8,128)S(1)}, f32[32,180]{1,0:T(8,128)S(1)}, u32[]{:S(2)}, u32[]{:S(2)}) %collective-permute-start.1) | collective-permute-done | bytes 23072 | tf_op jit(solution)/shard_map/ppermute | solution.py:130
  16.4 0.0 collective-permute-done
  16.4 0.6 gather_fusion
  17.0 0.4 fusion.67
  17.4 0.4 fusion.65
  17.9 1.1 %fusion.46 = f32[180,32,4]{0,1,2:T(8,128)S(1)} fusion(f32[32,180,4]{1,2,0:T(4,128)S(1)} %fusion.67, f32[32,180,4]{1,2,0:T(4,128)S(1)} %fusion.65, f32[180,4]{0,1:T(4,128)S(1)} %get-tuple-element.34, f32[180,4]{0,1:T(4,128)S(1)} %get-tuple-element.35), kind=kOutput, calls=%fused_computation.80 | convolution fusion | flops 50150160 | bytes 282240 | tf_op jit(solution)/shard_map/rbk,bj->rjk/dot_general | solution.py:101
  18.9 1.0 %fusion.50 = f32[180,32,4]{0,1,2:T(8,128)S(1)} fusion(f32[32,180,4]{1,2,0:T(4,128)S(1)} %fusion.67, f32[32,180,4]{1,2,0:T(4,128)S(1)} %fusion.65, f32[180,4]{0,1:T(4,128)S(1)} %get-tuple-element.34, f32[180,4]{0,1:T(4,128)S(1)} %get-tuple-element.35), kind=kOutput, calls=%fused_computation.84 | convolution fusion | flops 50150160 | bytes 282240 | tf_op jit(solution)/shard_map/rbk,bj->rjk/dot_general | solution.py:98
  20.0 1.1 %fusion.4 = f32[32,180,4]{1,0,2:T(8,128)S(1)} fusion(f32[180,32,4]{0,1,2:T(8,128)S(1)} %fusion.46, s32[180,4]{0,1:T(4,128)S(1)} %subtract_minimum_fusion, s32[32]{0:T(128)S(1)} %get-tuple-element.9, f32[32,180,4]{1,2,0:T(4,128)S(1)} %fusion.67, f32[32,180,4]{1,2,0:T(4,128)S(1)} %fusion.65, f32[180,4]{0,1:T(4,128)S(1)} %get-tuple-element.34, ...), kind=kOutput, calls=%fused_computation.9 | convolution fusion | flops 50219280 | bytes 377408 | tf_op jit(solution)/shard_map/rbk,bj->rjk/dot_general | solution.py:101
  21.0 1.0 %fusion.44 = f32[180,32,4]{0,1,2:T(8,128)S(1)} fusion(f32[32,180,4]{1,0,2:T(8,128)S(1)} %fusion.4), kind=kOutput, calls=%fused_computation.78 | convolution fusion | flops 50058000 | bytes 184320 | tf_op jit(solution)/shard_map/rjk,jb->rbk/dot_general | solution.py:112
  22.1 1.1 %fusion.6 = f32[32,180,4]{1,0,2:T(8,128)S(1)} fusion(f32[180,32,4]{0,1,2:T(8,128)S(1)} %fusion.50, s32[180,4]{0,1:T(4,128)S(1)} %subtract_minimum_fusion, s32[32]{0:T(128)S(1)} %get-tuple-element.9, f32[32,180,4]{1,2,0:T(4,128)S(1)} %fusion.67, f32[32,180,4]{1,2,0:T(4,128)S(1)} %fusion.65, f32[180,4]{0,1:T(4,128)S(1)} %get-tuple-element.34, ...), kind=kOutput, calls=%fused_computation.12 | convolution fusion | flops 50219280 | bytes 377408 | tf_op jit(solution)/shard_map/rbk,bj->rjk/dot_general | solution.py:98
  23.2 1.0 %fusion.48 = f32[180,32,4]{0,1,2:T(8,128)S(1)} fusion(f32[32,180,4]{1,0,2:T(8,128)S(1)} %fusion.6), kind=kOutput, calls=%fused_computation.82 | convolution fusion | flops 50058000 | bytes 184320 | tf_op jit(solution)/shard_map/rjk,jb->rbk/dot_general | solution.py:109
  24.2 1.0 %convolution_add_fusion = f32[180,32,4]{0,1,2:T(8,128)S(1)} fusion(f32[180,32,4]{0,1,2:T(8,128)S(1)} %fusion.44, f32[32,180,4]{1,0,2:T(8,128)S(1)} %fusion.6), kind=kOutput, calls=%fused_computation.5 | convolution fusion | flops 50081040 | bytes 276480 | tf_op jit(solution)/shard_map/rjk,jb->rbk/dot_general | solution.py:112
  25.3 1.1 %add_bitcast_fusion.2 = (f32[32,180,4]{1,0,2:T(8,128)S(1)}, f32[32,180,4]{1,0,2:T(8,128)S(1)}) fusion(f32[180,32,4]{0,1,2:T(8,128)S(1)} %convolution_add_fusion, f32[180,4]{0,1:T(4,128)S(1)} %get-tuple-element.34, f32[180,4]{0,1:T(4,128)S(1)} %get-tuple-element.35, f32[180,32,4]{0,1,2:T(8,128)S(1)} %fusion.48, f32[32,180,4]{1,0,2:T(8,128)S(1)} %fusion.4), kind=kOutput, calls=%fused_computation.111 | convolution fusion | flops 50219280 | bytes 466560 | tf_op jit(solution)/shard_map/rjk,jb->rbk/dot_general | solution.py:109
  26.3 0.4 fusion.70
  26.8 0.5 fusion.2
  27.2 0.7 %copy.37 = f32[32,4,180]{2,0,1:T(8,128)} copy(f32[32,4,180]{2,1,0:T(4,128)S(1)} %fusion.2) | data formatting | bytes 184320 | tf_op jit(solution)/shard_map/jit(_where)/select_n | solution.py:136
  27.9 3.3 %all-to-all-start = ((f32[32,4,180]{2,0,1:T(8,128)}), f32[32,4,180]{2,0,1:T(8,128)S(1)}, u32[]{:S(2)}, u32[]{:S(2)}) async-start(f32[32,4,180]{2,0,1:T(8,128)} %copy.37), calls=%async_computation | async-start | bytes 262144 | tf_op jit(solution)/shard_map/all_to_all | solution.py:137
  31.3 0.1 pad_maximum_fusion
  31.4 0.3 fusion.19
  31.7 0.2 slice_subtract_fusion
  32.0 5.6 %all-to-all-done = f32[32,4,180]{2,0,1:T(8,128)S(1)} async-done(((f32[32,4,180]{2,0,1:T(8,128)}), f32[32,4,180]{2,0,1:T(8,128)S(1)}, u32[]{:S(2)}, u32[]{:S(2)}) %all-to-all-start) | async-done | bytes 92192 | tf_op jit(solution)/shard_map/all_to_all | solution.py:137
  37.6 0.2 fusion.37
  37.7 1.7 %collective-permute-start.4 = (f32[4,5,32,3]{3,2,1,0:T(8,128)S(1)}, f32[4,5,32,3]{3,2,1,0:T(8,128)S(1)}, u32[]{:S(2)}, u32[]{:S(2)}) collective-permute-start(f32[4,5,32,3]{3,2,1,0:T(8,128)S(1)} %get-tuple-element.13), channel_id=1, source_target_pairs={{1,0},{2,1},{3,2},{0,3},{5,4},{6,5},{7,6},{4,7},{9,8},{10,9},{11,1... | collective-permute-start | bytes 23048 | tf_op jit(solution)/shard_map/ppermute | solution.py:29
  39.4 0.4 collective-permute-start.3
  39.8 0.4 fusion.12
  40.2 7.3 %collective-permute-done.4 = f32[4,5,32,3]{3,2,1,0:T(8,128)S(1)} collective-permute-done((f32[4,5,32,3]{3,2,1,0:T(8,128)S(1)}, f32[4,5,32,3]{3,2,1,0:T(8,128)S(1)}, u32[]{:S(2)}, u32[]{:S(2)}) %collective-permute-start.4) | collective-permute-done | bytes 7712 | tf_op jit(solution)/shard_map/ppermute | solution.py:29
  47.5 6.3 %collective-permute-done.3 = f32[4,5,32,3]{3,2,1,0:T(8,128)S(1)} collective-permute-done((f32[4,5,32,3]{3,2,1,0:T(8,128)S(1)}, f32[4,5,32,3]{3,2,1,0:T(8,128)S(1)}, u32[]{:S(2)}, u32[]{:S(2)}) %collective-permute-start.3) | collective-permute-done | bytes 7712 | tf_op jit(solution)/shard_map/ppermute | solution.py:27
  53.7 0.3 pad_maximum_fusion.5
  54.1 0.5 fusion.35
  54.6 0.3 slice_subtract_fusion.3
  55.0 0.1 compare_bitcast_fusion.1
  55.1 0.5 fusion.28
  55.6 1.0 %fusion.23 = f32[4,4,32,180]{3,2,1,0:T(8,128)} fusion(f32[4,4,32,180]{3,2,1,0:T(8,128)S(1)} %copy-done, f32[4,4,33,180]{3,2,1,0:T(8,128)S(1)} %fusion.12, f32[4,4,32,181]{3,2,1,0:T(8,128)S(1)} %fusion.28, f32[32]{0:T(128)S(1)} %fusion.134), kind=kLoop, calls=%fused_computation.45 | loop fusion | flops 460800 | bytes 2211968 | tf_op jit(solution)/shard_map/sub | solution.py:170
  56.6 0.7 %copy.68 = f32[4,32,180]{2,1,0:T(8,128)} copy(f32[4,32,180]{2,1,0:T(8,128)S(1)} %bitcast.98) | data formatting | bytes 184320
  (16 shorter events, 0.3 us)
Async XLA Ops:
  0.6 1.2 %copy-start = (f32[4,4,32,180]{3,2,1,0:T(8,128)S(1)}, f32[4,4,32,180]{3,2,1,0:T(8,128)}, u32[]{:S(2)}) copy-start(f32[4,4,32,180]{3,2,1,0:T(8,128)} %param.3) | copy-start | bytes 1105924
  1.8 29.4 %collective-permute-start.6 = (f32[4,5,3,180]{3,2,1,0:T(4,128)S(1)}, f32[4,5,3,180]{3,2,1,0:T(4,128)S(1)}, u32[]{:S(2)}, u32[]{:S(2)}) collective-permute-start(f32[4,5,3,180]{3,2,1,0:T(4,128)S(1)} %get-tuple-element.17), channel_id=1, source_target_pairs={{4,0},{8,4},{12,8},{16,12},{20,16},{24,20},{28,24},{5,1},{9,5},{13... | collective-permute-start | bytes 129608 | tf_op jit(solution)/shard_map/ppermute | solution.py:29
  3.1 28.1 %collective-permute-start.5 = (f32[4,5,3,180]{3,2,1,0:T(4,128)S(1)}, f32[4,5,3,180]{3,2,1,0:T(4,128)S(1)}, u32[]{:S(2)}, u32[]{:S(2)}) collective-permute-start(f32[4,5,3,180]{3,2,1,0:T(4,128)S(1)} %get-tuple-element.16), channel_id=1, source_target_pairs={{0,4},{4,8},{8,12},{12,16},{16,20},{20,24},{24,28},{1,5},{5,9},{9,... | collective-permute-start | bytes 129608 | tf_op jit(solution)/shard_map/ppermute | solution.py:27
  6.2 7.1 %collective-permute-start.2 = (f32[32,180]{1,0:T(8,128)S(1)}, f32[32,180]{1,0:T(8,128)S(1)}, u32[]{:S(2)}, u32[]{:S(2)}) collective-permute-start(f32[32,180]{1,0:T(8,128)S(1)} %get-tuple-element.31), channel_id=1, source_target_pairs={{0,3},{1,2},{2,1},{3,0},{4,7},{5,6},{6,5},{7,4},{8,11},{9,10},{10,... | collective-permute-start | bytes 69128 | tf_op jit(solution)/shard_map/ppermute | solution.py:130
  11.4 5.0 %collective-permute-start.1 = (f32[32,180]{1,0:T(8,128)S(1)}, f32[32,180]{1,0:T(8,128)S(1)}, u32[]{:S(2)}, u32[]{:S(2)}) collective-permute-start(f32[32,180]{1,0:T(8,128)S(1)} %get-tuple-element.32), channel_id=1, source_target_pairs={{0,2},{1,3},{2,0},{3,1},{4,6},{5,7},{6,4},{7,5},{8,10},{9,11},{10,... | collective-permute-start | bytes 69128 | tf_op jit(solution)/shard_map/ppermute | solution.py:130
  11.4 5.0 %collective-permute-start = (f32[32,180]{1,0:T(8,128)S(1)}, f32[32,180]{1,0:T(8,128)S(1)}, u32[]{:S(2)}, u32[]{:S(2)}) collective-permute-start(f32[32,180]{1,0:T(8,128)S(1)} %get-tuple-element.33), channel_id=1, source_target_pairs={{0,1},{1,0},{2,3},{3,2},{4,5},{5,4},{6,7},{7,6},{8,9},{9,8},{10,11... | collective-permute-start | bytes 69128 | tf_op jit(solution)/shard_map/ppermute | solution.py:130
  12.2 0.7 %copy-start.1 = (s32[256]{0:T(256)S(1)}, s32[256]{0:T(256)}, u32[]{:S(2)}) copy-start(s32[256]{0:T(256)} %param.5) | copy-start | bytes 3076
  27.9 9.6 %all-to-all-start = ((f32[32,4,180]{2,0,1:T(8,128)}), f32[32,4,180]{2,0,1:T(8,128)S(1)}, u32[]{:S(2)}, u32[]{:S(2)}) async-start(f32[32,4,180]{2,0,1:T(8,128)} %copy.37), calls=%async_computation | async-start | bytes 262144 | tf_op jit(solution)/shard_map/all_to_all | solution.py:137
  37.7 9.8 %collective-permute-start.4 = (f32[4,5,32,3]{3,2,1,0:T(8,128)S(1)}, f32[4,5,32,3]{3,2,1,0:T(8,128)S(1)}, u32[]{:S(2)}, u32[]{:S(2)}) collective-permute-start(f32[4,5,32,3]{3,2,1,0:T(8,128)S(1)} %get-tuple-element.13), channel_id=1, source_target_pairs={{1,0},{2,1},{3,2},{0,3},{5,4},{6,5},{7,6},{4,7},{9,8},{10,9},{11,1... | collective-permute-start | bytes 23048 | tf_op jit(solution)/shard_map/ppermute | solution.py:29
  39.4 14.4 %collective-permute-start.3 = (f32[4,5,32,3]{3,2,1,0:T(8,128)S(1)}, f32[4,5,32,3]{3,2,1,0:T(8,128)S(1)}, u32[]{:S(2)}, u32[]{:S(2)}) collective-permute-start(f32[4,5,32,3]{3,2,1,0:T(8,128)S(1)} %get-tuple-element.12), channel_id=1, source_target_pairs={{0,1},{1,2},{2,3},{3,0},{4,5},{5,6},{6,7},{7,4},{8,9},{9,10},{10,1... | collective-permute-start | bytes 23048 | tf_op jit(solution)/shard_map/ppermute | solution.py:27
